TPU v7x, 512 devices: a whole 4x8x8 slice. The times are simulated.
512 devices in a mesh: row: 16 (over z, core), col: 32 (over x, y).
Axes of the slice: x: 4, y: 8, z: 8, core: 2. Of those that a mesh axis runs over, the one named last changes fastest.
Arguments:
- u_front: bfloat16 [2, 2048, 25, 2048], P(None, 'col', None, 'row'), may hold values from -0.02734375 to 0.02734375
- inverse_blocks: bfloat16 [2, 2048, 1, 2048], P(None, 'col', None, 'row')
- rhs_window: float32 [32, 2, 2048], P(None, None, 'col'), may hold values from -6 to 6
- pivot_inverse: float32 [2, 2048], P(None, 'col'), may hold values from 0.25 to 4
- below_solution: bfloat16 [32, 23, 2048], P(None, None, 'row'), may hold values from -6 to 6
- u_child: bfloat16 [4096, 16, 2048], P('col', None, 'row'), may hold values from -0.03125 to 0.03125
- rhs_child: float32 [32, 4096], P(None, 'col'), may hold values from -6 to 6
- child_map: int32 [2, 256], replicated, may hold values from 0 to 399, as said below
- child_counts: int32 [2], replicated, may hold values from 128 to 256, as said below
Outputs:
- x_window: float32 [32, 2, 2048], P(None, None, 'row')
- child_out: float32 [32, 4096], P(None, 'col')
Inputs may be any that keep to these rules, and one draw needn't show every extreme that they name: Slot s of a child lies on row index s % 16 of the child's rows, and the block it names lies on row index (s % 16 + s // 16) % 16 of the front's rows, that is child_map[h, s] % 16 equals that number; one child names each block at most once; both ends of the range are named. `child_counts`: one of the two children uses all 256 slots.
All inputs are finite; a program needn't handle non-finite values.
Results may differ from a plain program's by a relative error of at most 0.003.
Values may be sent and summed in bfloat16 or wider, within the bound.
A program may use at most 64 MiB of HBM per device.

v0:
```python
import jax
import jax.numpy as jnp
from jax import lax
from jax.sharding import PartitionSpec as P


def local(
    u_front,
    inverse_blocks,
    rhs_window,
    pivot_inverse,
    below_solution,
    u_child,
    rhs_child,
    child_map,
    child_counts,
):
    panel_count = u_front.shape[0]
    front_blocks = u_front.shape[2]
    block_rows = u_front.shape[3]
    panel_blocks = inverse_blocks.shape[2]
    window_blocks = panel_count * panel_blocks
    rhs_count = rhs_window.shape[0]
    scaled = rhs_window * pivot_inverse[None]
    solved = [None] * panel_count
    solved_rows = jnp.concatenate(
        [jnp.zeros((rhs_count, window_blocks, block_rows), jnp.bfloat16), below_solution], axis=1
    )
    for panel_index in reversed(range(panel_count)):
        partial_value = jnp.einsum(
            "wqb,nqb->nw", u_front[panel_index], solved_rows, preferred_element_type=jnp.float32
        )
        summed = lax.psum(partial_value, "row")
        reduced = (scaled[:, panel_index] - summed).astype(jnp.bfloat16)
        partial_share = jnp.einsum(
            "nw,wpb->npb", reduced, inverse_blocks[panel_index], preferred_element_type=jnp.float32
        )
        result = lax.psum(partial_share, "col")
        solved[panel_index] = result
        lower_edge = panel_index * panel_blocks
        solved_rows = lax.dynamic_update_slice_in_dim(
            solved_rows, result.astype(jnp.bfloat16), lower_edge, 1
        )
    x_window = jnp.concatenate(solved, axis=1)
    row_count = lax.axis_size("row")
    my_row = lax.axis_index("row")
    half_width = lax.axis_size("col") // 2
    which_child = lax.axis_index("col") // half_width
    slot_depth = u_child.shape[1]
    child_slots = child_map[which_child]
    local_slots = jnp.arange(slot_depth, dtype=jnp.int32) * row_count + my_row
    wanted = child_slots[local_slots]
    live_mask = (local_slots < child_counts[which_child]).astype(jnp.bfloat16)
    section = lax.all_gather(solved_rows, "row", axis=1, tiled=True)
    length = section.shape[1]
    gathered_index = jnp.arange(length, dtype=jnp.int32)
    global_block = gathered_index % front_blocks * row_count + gathered_index // front_blocks
    selector = (wanted[:, None] == global_block[None, :]).astype(jnp.bfloat16)
    incoming = jnp.einsum(
        "sq,nqb->nsb", selector, section, preferred_element_type=jnp.float32
    ).astype(jnp.bfloat16)
    masked = incoming * live_mask[None, :, None]
    child_part = jnp.einsum("psb,nsb->np", u_child, masked, preferred_element_type=jnp.float32)
    child_total = lax.psum(child_part, "row")
    child_out = rhs_child - child_total
    return (x_window, child_out)


def solution(mesh):
    return jax.shard_map(
        local,
        mesh=mesh,
        in_specs=(
            P(None, "col", None, "row"),
            P(None, "col", None, "row"),
            P(None, None, "col"),
            P(None, "col"),
            P(None, None, "row"),
            P("col", None, "row"),
            P(None, "col"),
            P(),
            P(),
        ),
        out_specs=(P(None, None, "row"), P(None, "col")),
        check_vma=False,
    )
```

profile of v0, /device:TPU:2, one launch (start us, length us, event | category | flops | bytes accessed | tf_op | source)
XLA Modules:
  0.0 485.7 jit_solution(11730641307680731013)
XLA Ops:
  7.2 0.0 copy-start
  7.2 0.0 all-gather.2.cloned.1.call-start
  7.2 1.4 convolution_bitcast_fusion.3
  8.6 54.0 %psum.35 = f32[32,64]{1,0:T(8,128)S(1)} all-reduce(f32[32,64]{1,0:T(8,128)S(1)} %convolution_bitcast_fusion.3), channel_id=1, replica_groups=mesh['row'=16,'col'=32] {'row'}, use_global_device_ids=true, to_apply=%region_0.0 | all-reduce | flops 2048 | bytes 16384 | tf_op jit(solution)/shard_map/psum | solution.py:33
  62.6 0.8 copy_multiply_fusion
  63.4 0.8 convolution_bitcast_fusion.2
  64.3 131.2 %psum.36 = f32[32,1,128]{2,0,1:T(8,128)S(1)} all-reduce(f32[32,1,128]{2,0,1:T(8,128)S(1)} %convolution_bitcast_fusion.2), channel_id=1, replica_groups=mesh['row'=16,'col'=32] {'col'}, use_global_device_ids=true, to_apply=%region_1.0 | all-reduce | flops 4096 | bytes 32768 | tf_op jit(solution)/shard_map/psum | solution.py:38
  195.5 0.9 concatenate.6
  196.4 0.0 copy-start.2
  196.4 1.2 convolution_bitcast_fusion.4
  197.7 45.7 %psum.37 = f32[32,64]{1,0:T(8,128)S(1)} all-reduce(f32[32,64]{1,0:T(8,128)S(1)} %convolution_bitcast_fusion.4), channel_id=1, replica_groups=mesh['row'=16,'col'=32] {'row'}, use_global_device_ids=true, to_apply=%region_2.0 | all-reduce | flops 2048 | bytes 16384 | tf_op jit(solution)/shard_map/psum | solution.py:33
  243.4 0.8 convolution_bitcast_fusion.1
  244.2 137.7 %psum.38 = f32[32,1,128]{2,0,1:T(8,128)S(1)} all-reduce(f32[32,1,128]{2,0,1:T(8,128)S(1)} %convolution_bitcast_fusion.1), channel_id=1, replica_groups=mesh['row'=16,'col'=32] {'col'}, use_global_device_ids=true, to_apply=%region_3.0 | all-reduce | flops 4096 | bytes 32768 | tf_op jit(solution)/shard_map/psum | solution.py:38
  381.9 0.0 copy-start.1
  381.9 0.7 copy-done.1
  382.6 0.0 all-gather.2.cloned.1.call-update
  382.6 0.6 copy.19
  383.3 1.2 dynamic_slice.7
  384.5 0.7 constant_dynamic-slice_fusion
  385.2 0.7 gather_fusion
  385.9 0.7 compare_convert_fusion
  386.5 41.5 %all-gather.2.cloned.1.call-done = bf16[32,400,128]{2,0,1:T(8,128)(2,1)} async-done(((bf16[32,25,128]{2,0,1:T(8,128)(2,1)}), bf16[32,400,128]{2,0,1:T(8,128)(2,1)}) %all-gather.2.cloned.1.call-update) | async-done | bytes 3276816 | tf_op jit(solution)/shard_map/all_gather | solution.py:54
  428.1 2.9 fusion.8
  431.0 0.0 copy-done
  431.0 0.3 convolution_bitcast_fusion
  431.2 47.0 %psum.39 = f32[32,128]{1,0:T(8,128)S(1)} all-reduce(f32[32,128]{1,0:T(8,128)S(1)} %convolution_bitcast_fusion), channel_id=1, replica_groups=mesh['row'=16,'col'=32] {'row'}, use_global_device_ids=true, to_apply=%region_4.5 | all-reduce | flops 4096 | bytes 32768 | tf_op jit(solution)/shard_map/psum | solution.py:64
  478.3 0.0 copy-done.2
  478.3 0.6 sub.23
  (6 shorter events, 0.0 us)
Async XLA Ops:
  7.2 423.8 %copy-start = (bf16[128,16,128]{2,1,0:T(8,128)(2,1)S(1)}, bf16[128,16,128]{2,1,0:T(8,128)(2,1)}, u32[]{:S(2)}) copy-start(bf16[128,16,128]{2,1,0:T(8,128)(2,1)} %param.14) | copy-start | bytes 1572868
  7.2 420.9 %all-gather.2.cloned.1.call-start = ((), (), s32[]{:S(2)}) async-start(), calls=%async_computation | async-start | bytes 3481600 | tf_op jit(solution)/shard_map/all_gather | solution.py:54
  196.4 281.9 %copy-start.2 = (f32[32,128]{1,0:T(8,128)S(1)}, f32[32,128]{1,0:T(8,128)}, u32[]{:S(2)}) copy-start(f32[32,128]{1,0:T(8,128)} %param.15) | copy-start | bytes 49156
  381.9 0.7 copy-start.1
Sparse Core Ops, SparseCore 0:
  382.7 45.3 all-gather.1
where the time goes:
time: 486 us
  blocking collectives  416 us (86%)
  waiting for transfers between devices  41.5 us (9%)
  between operations  14.1 us (3%)
  matrix products  7.46 us (2%)
  local copies, waits for them, and re-layouts  4.87 us (1%)
    psum x2, blocking collectives, local(): result = lax.psum(partial_share, 'col')  269 us
    psum x2, blocking collectives, local(): summed = lax.psum(partial_value, 'row')  99.7 us
    psum x1, blocking collectives, local(): child_total = lax.psum(child_part, 'row')  47 us
    all_gather x1, waiting for transfers between devices, local(): section = lax.all_gather(solved_rows, 'row', axis=1, tiled=True)  41.5 us
  transfers between devices with their start and end apart: 1, of which 1 were waited for; matrix products, arithmetic and copies ran while one was open for 1% of the time, Pallas kernels for 0%

commit v1 on v0

--- a/solution.py
+++ b/solution.py
@@ -51,7 +51,9 @@
     local_slots = jnp.arange(slot_depth, dtype=jnp.int32) * row_count + my_row
     wanted = child_slots[local_slots]
     live_mask = (local_slots < child_counts[which_child]).astype(jnp.bfloat16)
-    section = lax.all_gather(solved_rows, "row", axis=1, tiled=True)
+    section = jnp.concatenate(
+        lax.all_to_all(jnp.stack([solved_rows] * lax.axis_size("row")), "row", 0, 0), axis=1
+    )
     length = section.shape[1]
     gathered_index = jnp.arange(length, dtype=jnp.int32)
     global_block = gathered_index % front_blocks * row_count + gathered_index // front_blocks

time: 486 us -> 518 us (1.066)
  the two profiles are of different devices: /device:TPU:2 before, /device:TPU:1 now
where the time goes in v1:
time: 518 us
  blocking collectives  395 us (76%)
  waiting for transfers between devices  71.4 us (14%)
  starting transfers between devices  35.2 us (7%)
  matrix products  7.45 us (1%)
  local copies, waits for them, and re-layouts  5.76 us (1%)
    psum x2, blocking collectives, local(): result = lax.psum(partial_share, 'col')  226 us
    psum x2, blocking collectives, local(): summed = lax.psum(partial_value, 'row')  125 us
    all_to_all x1, waiting for transfers between devices, local(): lax.all_to_all(jnp.stack([solved_rows] * lax.axis_size('row')), 'row', 0, 0)  71.4 us
    psum x1, blocking collectives, local(): child_total = lax.psum(child_part, 'row')  43.5 us
    all_to_all x1, starting transfers between devices, local(): lax.all_to_all(jnp.stack([solved_rows] * lax.axis_size('row')), 'row', 0, 0)  35.2 us
  transfers between devices with their start and end apart: 1, of which 1 were waited for; matrix products, arithmetic and copies ran while one was open for 0% of the time, Pallas kernels for 0%

profile of v1, /device:TPU:1, one launch (start us, length us, event | category | flops | bytes accessed | tf_op | source)
XLA Modules:
  0.0 517.5 jit_solution(8953386282456057238)
XLA Ops:
  0.6 0.0 copy-start
  0.6 0.7 broadcast.111
  1.4 0.8 broadcast_multiply_fusion
  2.2 1.3 convolution_bitcast_fusion.3
  3.5 52.0 %psum.35 = f32[32,64]{1,0:T(8,128)S(1)} all-reduce(f32[32,64]{1,0:T(8,128)S(1)} %convolution_bitcast_fusion.3), channel_id=1, replica_groups=mesh['row'=16,'col'=32] {'row'}, use_global_device_ids=true, to_apply=%region_0.0 | all-reduce | flops 2048 | bytes 16384 | tf_op jit(solution)/shard_map/psum | solution.py:33
  55.5 0.8 convolution_bitcast_fusion.2
  56.4 115.7 %psum.36 = f32[32,1,128]{2,0,1:T(8,128)S(1)} all-reduce(f32[32,1,128]{2,0,1:T(8,128)S(1)} %convolution_bitcast_fusion.2), channel_id=1, replica_groups=mesh['row'=16,'col'=32] {'col'}, use_global_device_ids=true, to_apply=%region_1.0 | all-reduce | flops 4096 | bytes 32768 | tf_op jit(solution)/shard_map/psum | solution.py:38
  172.1 0.9 concatenate.6
  173.0 1.2 convolution_bitcast_fusion.4
  174.3 73.3 %psum.37 = f32[32,64]{1,0:T(8,128)S(1)} all-reduce(f32[32,64]{1,0:T(8,128)S(1)} %convolution_bitcast_fusion.4), channel_id=1, replica_groups=mesh['row'=16,'col'=32] {'row'}, use_global_device_ids=true, to_apply=%region_2.0 | all-reduce | flops 2048 | bytes 16384 | tf_op jit(solution)/shard_map/psum | solution.py:33
  247.6 0.8 convolution_bitcast_fusion.1
  248.4 110.3 %psum.38 = f32[32,1,128]{2,0,1:T(8,128)S(1)} all-reduce(f32[32,1,128]{2,0,1:T(8,128)S(1)} %convolution_bitcast_fusion.1), channel_id=1, replica_groups=mesh['row'=16,'col'=32] {'col'}, use_global_device_ids=true, to_apply=%region_3.0 | all-reduce | flops 4096 | bytes 32768 | tf_op jit(solution)/shard_map/psum | solution.py:38
  358.8 2.1 stack.2
  360.9 0.0 copy-start.3
  360.9 0.0 copy-start.2
  360.9 35.2 %all-to-all-start = ((bf16[16,32,25,128]{3,1,2,0:T(8,128)(2,1)}), bf16[16,32,25,128]{3,1,2,0:T(8,128)(2,1)}, u32[]{:S(2)}, u32[]{:S(2)}) async-start(bf16[16,32,25,128]{3,1,2,0:T(8,128)(2,1)} %stack.2), calls=%async_computation | async-start | bytes 6553600 | tf_op jit(solution)/shard_map/all_to_all | solution.py:55
  396.1 0.0 copy-start.1
  396.1 0.6 copy.15
  396.8 0.0 copy-done.3
  396.8 0.6 dynamic_slice.7
  397.4 0.0 copy-done.2
  397.4 0.7 gather_fusion
  398.1 0.7 compare_convert_fusion
  398.7 71.4 %all-to-all-done = bf16[16,32,25,128]{3,1,2,0:T(8,128)(2,1)} async-done(((bf16[16,32,25,128]{3,1,2,0:T(8,128)(2,1)}), bf16[16,32,25,128]{3,1,2,0:T(8,128)(2,1)}, u32[]{:S(2)}, u32[]{:S(2)}) %all-to-all-start) | async-done | bytes 3276832 | tf_op jit(solution)/shard_map/all_to_all | solution.py:55
  470.1 2.9 fusion
  473.0 0.0 copy-done
  473.0 0.3 convolution_bitcast_fusion
  473.4 43.5 %psum.39 = f32[32,128]{1,0:T(8,128)S(1)} all-reduce(f32[32,128]{1,0:T(8,128)S(1)} %convolution_bitcast_fusion), channel_id=1, replica_groups=mesh['row'=16,'col'=32] {'row'}, use_global_device_ids=true, to_apply=%region_4.5 | all-reduce | flops 4096 | bytes 32768 | tf_op jit(solution)/shard_map/psum | solution.py:66
  516.9 0.0 copy-done.1
  516.9 0.6 sub.23
  (8 shorter events, 0.1 us)
Async XLA Ops:
  0.6 472.4 %copy-start = (bf16[128,16,128]{2,1,0:T(8,128)(2,1)S(1)}, bf16[128,16,128]{2,1,0:T(8,128)(2,1)}, u32[]{:S(2)}) copy-start(bf16[128,16,128]{2,1,0:T(8,128)(2,1)} %param.14) | copy-start | bytes 1572868
  360.9 35.9 %copy-start.3 = (s32[2]{0:T(128)S(1)}, s32[2]{0:T(128)}, u32[]{:S(2)}) copy-start(s32[2]{0:T(128)} %param.17) | copy-start | bytes 28
  360.9 36.5 %copy-start.2 = (s32[2,256]{1,0:T(2,128)S(1)}, s32[2,256]{1,0:T(2,128)}, u32[]{:S(2)}) copy-start(s32[2,256]{1,0:T(2,128)} %param.16) | copy-start | bytes 6148
  360.9 109.2 %all-to-all-start = ((bf16[16,32,25,128]{3,1,2,0:T(8,128)(2,1)}), bf16[16,32,25,128]{3,1,2,0:T(8,128)(2,1)}, u32[]{:S(2)}, u32[]{:S(2)}) async-start(bf16[16,32,25,128]{3,1,2,0:T(8,128)(2,1)} %stack.2), calls=%async_computation | async-start | bytes 6553600 | tf_op jit(solution)/shard_map/all_to_all | solution.py:55
  396.1 120.8 %copy-start.1 = (f32[32,128]{1,0:T(8,128)S(1)}, f32[32,128]{1,0:T(8,128)}, u32[]{:S(2)}) copy-start(f32[32,128]{1,0:T(8,128)} %param.15) | copy-start | bytes 49156

commit v2 on v0

--- a/solution.py
+++ b/solution.py
@@ -35,7 +35,7 @@
         partial_share = jnp.einsum(
             "nw,wpb->npb", reduced, inverse_blocks[panel_index], preferred_element_type=jnp.float32
         )
-        result = lax.psum(partial_share, "col")
+        result = jnp.sum(lax.all_gather(partial_share, "col"), axis=0)
         solved[panel_index] = result
         lower_edge = panel_index * panel_blocks
         solved_rows = lax.dynamic_update_slice_in_dim(

time: 486 us -> 309 us (0.64)
  blocking collectives: 416 us -> 244 us
    psum x2 -> x0, blocking collectives: 269 us -> none  [local(): result = lax.psum(partial_share, 'col')]
    all_gather x0 -> x2, blocking collectives: none -> 97.2 us  [local(): result = jnp.sum(lax.all_gather(partial_share, 'col'), axis=0)]
where the time goes in v2:
time: 309 us; the launch traced here: 308 us
  blocking collectives  244 us (79%)
  waiting for transfers between devices  36.8 us (12%)
  between operations  14.1 us (5%)
  matrix products  7.46 us (2%)
  local copies, waits for them, and re-layouts  3.53 us (1%)
    psum x2, blocking collectives, local(): summed = lax.psum(partial_value, 'row')  99.7 us
    all_gather x2, blocking collectives, local(): result = jnp.sum(lax.all_gather(partial_share, 'col'), axis=0)  97.2 us
    psum x1, blocking collectives, local(): child_total = lax.psum(child_part, 'row')  47 us
    all_gather x1, waiting for transfers between devices, local(): section = lax.all_gather(solved_rows, 'row', axis=1, tiled=True)  36.7 us
  transfers between devices with their start and end apart: 1, of which 1 were waited for; matrix products, arithmetic and copies ran while one was open for 1% of the time, Pallas kernels for 0%

profile of v2, /device:TPU:2, one launch (start us, length us, event | category | flops | bytes accessed | tf_op | source)
XLA Modules:
  0.0 308.1 jit_solution(13128495248027180070)
XLA Ops:
  7.2 0.0 copy-start
  7.2 0.0 copy-start.4
  7.2 0.0 copy-start.3
  7.2 0.0 all-gather.4.cloned.1.call-start
  7.2 1.4 convolution_bitcast_fusion.1
  8.6 54.0 %psum.21 = f32[32,64]{1,0:T(8,128)S(1)} all-reduce(f32[32,64]{1,0:T(8,128)S(1)} %convolution_bitcast_fusion.1), channel_id=1, replica_groups=mesh['row'=16,'col'=32] {'row'}, use_global_device_ids=true, to_apply=%region_0.0 | all-reduce | flops 2048 | bytes 16384 | tf_op jit(solution)/shard_map/psum | solution.py:33
  62.7 0.8 copy_multiply_fusion
  63.4 0.8 fusion.25
  64.3 49.6 %all-gather = f32[1024,128]{1,0:T(8,128)S(1)} all-gather(f32[32,128]{1,0:T(8,128)S(1)} %fusion.25), channel_id=2, replica_groups=mesh['row'=16,'col'=32] {'col'}, dimensions={0}, use_global_device_ids=true | all-gather | bytes 540672 | tf_op jit(solution)/shard_map/all_gather | solution.py:38
  113.9 0.9 concatenate.6
  114.9 1.2 convolution_bitcast_fusion.2
  116.2 45.7 %psum.22 = f32[32,64]{1,0:T(8,128)S(1)} all-reduce(f32[32,64]{1,0:T(8,128)S(1)} %convolution_bitcast_fusion.2), channel_id=1, replica_groups=mesh['row'=16,'col'=32] {'row'}, use_global_device_ids=true, to_apply=%region_2.0 | all-reduce | flops 2048 | bytes 16384 | tf_op jit(solution)/shard_map/psum | solution.py:33
  161.9 0.8 fusion.23
  162.7 47.6 %all-gather.1 = f32[1024,128]{1,0:T(8,128)S(1)} all-gather(f32[32,128]{1,0:T(8,128)S(1)} %fusion.23), channel_id=3, replica_groups=mesh['row'=16,'col'=32] {'col'}, dimensions={0}, use_global_device_ids=true | all-gather | bytes 540672 | tf_op jit(solution)/shard_map/all_gather | solution.py:38
  210.3 0.0 copy-start.2
  210.3 0.0 copy-start.1
  210.3 0.7 copy-done.1
  211.0 0.0 all-gather.4.cloned.1.call-update
  211.1 0.6 copy.21
  211.7 0.0 copy-done.4
  211.7 0.6 dynamic_slice.7
  212.3 0.0 copy-done.3
  212.3 0.7 gather_fusion
  213.0 0.7 compare_convert_fusion
  213.7 36.7 %all-gather.4.cloned.1.call-done = bf16[32,400,128]{2,0,1:T(8,128)(2,1)} async-done(((bf16[32,25,128]{2,0,1:T(8,128)(2,1)}), bf16[32,400,128]{2,0,1:T(8,128)(2,1)}) %all-gather.4.cloned.1.call-update) | async-done | bytes 3276816 | tf_op jit(solution)/shard_map/all_gather | solution.py:54
  250.4 2.9 fusion.8
  253.3 0.0 copy-done
  253.3 0.3 convolution_bitcast_fusion
  253.6 47.0 %psum.23 = f32[32,128]{1,0:T(8,128)S(1)} all-reduce(f32[32,128]{1,0:T(8,128)S(1)} %convolution_bitcast_fusion), channel_id=1, replica_groups=mesh['row'=16,'col'=32] {'row'}, use_global_device_ids=true, to_apply=%region_4.5 | all-reduce | flops 4096 | bytes 32768 | tf_op jit(solution)/shard_map/psum | solution.py:64
  300.6 0.0 copy-done.2
  300.6 0.6 sub.23
  (9 shorter events, 0.1 us)
Async XLA Ops:
  7.2 246.1 %copy-start = (bf16[128,16,128]{2,1,0:T(8,128)(2,1)S(1)}, bf16[128,16,128]{2,1,0:T(8,128)(2,1)}, u32[]{:S(2)}) copy-start(bf16[128,16,128]{2,1,0:T(8,128)(2,1)} %param.14) | copy-start | bytes 1572868
  7.2 204.5 %copy-start.4 = (s32[2]{0:T(128)S(1)}, s32[2]{0:T(128)}, u32[]{:S(2)}) copy-start(s32[2]{0:T(128)} %param.17) | copy-start | bytes 28
  7.2 205.1 %copy-start.3 = (s32[2,256]{1,0:T(2,128)S(1)}, s32[2,256]{1,0:T(2,128)}, u32[]{:S(2)}) copy-start(s32[2,256]{1,0:T(2,128)} %param.16) | copy-start | bytes 6148
  7.2 243.2 %all-gather.4.cloned.1.call-start = ((), (), s32[]{:S(2)}) async-start(), calls=%async_computation | async-start | bytes 3481600 | tf_op jit(solution)/shard_map/all_gather | solution.py:54
  210.3 90.4 %copy-start.2 = (f32[32,128]{1,0:T(8,128)S(1)}, f32[32,128]{1,0:T(8,128)}, u32[]{:S(2)}) copy-start(f32[32,128]{1,0:T(8,128)} %param.15) | copy-start | bytes 49156
  210.3 0.7 copy-start.1
Sparse Core Ops, SparseCore 0:
  211.2 39.2 all-gather.3
